TPU v7x, 32 devices: a whole 2x2x4 slice. The times are simulated.
32 devices in a mesh: dp: 4 (over x, core), expert: 8 (over z, y).
Axes of the slice: x: 2, y: 2, z: 4, core: 2. Of those that a mesh axis runs over, the one named last changes fastest.
Arguments:
- tokens: bfloat16 [6144, 1024], P(('dp', 'expert')), may hold values from -6 to 6
- norm_gain: float32 [1024], replicated, may hold values from 0.5 to 1.5
- expert_ids: int32 [6144, 2], P(('dp', 'expert')), may hold values from 0 to 7, all different within a row; in each aligned block of 192 rows (0 to 191, 192 to 383, ...) at most 72 rows name the same one
- gate_share: float32 [6144, 2], P(('dp', 'expert')), may hold values from 0.25 to 1
- w_gate: bfloat16 [8, 2048, 1024], P('expert', 'dp'), may hold values from -0.1875 to 0.1875
- w_up: bfloat16 [8, 2048, 1024], P('expert', 'dp'), may hold values from -0.1875 to 0.1875
- w_down: bfloat16 [8, 2048, 1024], P('expert', 'dp'), may hold values from -0.125 to 0.125
- out_grad: bfloat16 [6144, 1024], P(('dp', 'expert')), may hold values from -6 to 6
Outputs:
- mixed: bfloat16 [6144, 1024], P(('dp', 'expert'))
- tokens_grad: bfloat16 [6144, 1024], P(('dp', 'expert'))
- gain_grad: float32 [1024], replicated
- w_gate_grad: float32 [8, 2048, 1024], P('expert', 'dp')
- w_up_grad: float32 [8, 2048, 1024], P('expert', 'dp')
- w_down_grad: float32 [8, 2048, 1024], P('expert', 'dp')
Inputs may be any that keep to these rules, and one draw needn't show every extreme that they name: `expert_ids`: each token names two different experts. In each aligned block of 192 rows (the rows of one device) no expert is named more than 72 times, a bound that some block reaches.
All inputs are finite; a program needn't handle non-finite values.
Results may differ from a plain program's by a relative error of at most 0.0095.
Values may be sent and summed in bfloat16 or wider, within the bound.
A program may use at most 128 MiB of HBM per device.

v0:
```python
import jax
import jax.numpy as jnp
from jax import lax
from jax.sharding import PartitionSpec as P

epsilon = 1e-05
contract_last = (((1,), (1,)), ((), ()))
contract_first = (((0,), (0,)), ((), ()))


def pair_slots(expert_block, experts_n, capacity):
    flat_ids = expert_block.reshape(-1)
    onehot = (flat_ids[:, None] == jnp.arange(experts_n, dtype=jnp.int32)[None, :]).astype(
        jnp.int32
    )
    earlier = jnp.cumsum(onehot, axis=0) - onehot
    rank_ids = jnp.sum(earlier * onehot, axis=1)
    return flat_ids * capacity + rank_ids


def expert_inner(in_rows, cot_rows, gate_weight, up_weight, down_weight):
    gate_pre = lax.dot_general(
        in_rows, gate_weight, contract_last, preferred_element_type=jnp.float32
    )
    up_pre = lax.dot_general(in_rows, up_weight, contract_last, preferred_element_type=jnp.float32)
    sigmoid_gate = jax.nn.sigmoid(gate_pre)
    activated = gate_pre * sigmoid_gate
    hidden = (activated * up_pre).astype(jnp.bfloat16)
    hidden_grad = lax.dot_general(
        cot_rows, down_weight, contract_last, preferred_element_type=jnp.float32
    )
    up_grad = (hidden_grad * activated).astype(jnp.bfloat16)
    gate_grad = (
        hidden_grad * up_pre * sigmoid_gate * (1.0 + gate_pre * (1.0 - sigmoid_gate))
    ).astype(jnp.bfloat16)
    return (hidden, gate_grad, up_grad)


def expert_outer(hidden, gate_grad, up_grad, gate_weight, up_weight, down_weight):
    out_part = jnp.dot(hidden, down_weight, preferred_element_type=jnp.float32)
    input_part = jnp.dot(gate_grad, gate_weight, preferred_element_type=jnp.float32) + jnp.dot(
        up_grad, up_weight, preferred_element_type=jnp.float32
    )
    return (out_part, input_part)


def contract_rows(left, right):
    return lax.dot_general(left, right, contract_first, preferred_element_type=jnp.float32)


def on_device(tokens, norm_gain, expert_ids, gate_share, w_gate, w_up, w_down, out_grad):
    tok_rows, feature_width = tokens.shape
    experts_n = lax.axis_size("expert")
    capacity = 3 * tok_rows // experts_n
    slot_count = experts_n * capacity
    tok_float = tokens.astype(jnp.float32)
    inv_rms = lax.rsqrt(jnp.mean(tok_float * tok_float, axis=1, keepdims=True) + epsilon)
    normed = (tok_float * inv_rms * norm_gain[None, :]).astype(jnp.bfloat16)
    pair_cot = (
        (gate_share[:, :, None] * out_grad.astype(jnp.float32)[:, None, :])
        .astype(jnp.bfloat16)
        .reshape(2 * tok_rows, feature_width)
    )
    slot_ids = pair_slots(expert_ids, experts_n, capacity)
    matches = jnp.arange(slot_count, dtype=jnp.int32)[:, None] == slot_ids[None, :]
    pair_place = matches.astype(jnp.bfloat16)
    token_place = jnp.any(matches.reshape(slot_count, tok_rows, 2), axis=2).astype(jnp.bfloat16)
    send_rows = jnp.dot(token_place, normed, preferred_element_type=jnp.float32).astype(
        jnp.bfloat16
    )
    send_cot = jnp.dot(pair_place, pair_cot, preferred_element_type=jnp.float32).astype(
        jnp.bfloat16
    )
    in_rows, cot_rows = (
        lax.all_to_all(send_rows, "expert", split_axis=0, concat_axis=0, tiled=True),
        lax.all_to_all(send_cot, "expert", split_axis=0, concat_axis=0, tiled=True),
    )
    gate_own, up_own, down_own = (w_gate[0], w_up[0], w_down[0])
    gate_all, up_all, down_all = (
        lax.all_gather(gate_own, "dp", axis=0, tiled=True),
        lax.all_gather(up_own, "dp", axis=0, tiled=True),
        lax.all_gather(down_own, "dp", axis=0, tiled=True),
    )
    hidden, gate_grad, up_grad = expert_inner(in_rows, cot_rows, gate_all, up_all, down_all)
    out_part, input_part = expert_outer(hidden, gate_grad, up_grad, gate_all, up_all, down_all)
    out_rows = out_part.astype(jnp.bfloat16)
    input_rows = input_part.astype(jnp.bfloat16)
    gradients = lax.psum_scatter(
        jnp.concatenate(
            [
                contract_rows(gate_grad, in_rows),
                contract_rows(up_grad, in_rows),
                contract_rows(hidden, cot_rows),
            ],
            axis=1,
        ).astype(jnp.bfloat16),
        "dp",
        scatter_dimension=0,
        tiled=True,
    ).astype(jnp.float32)
    back_out, back_input = (
        lax.all_to_all(out_rows, "expert", split_axis=0, concat_axis=0, tiled=True),
        lax.all_to_all(input_rows, "expert", split_axis=0, concat_axis=0, tiled=True),
    )
    out_pairs = contract_rows(pair_place, back_out).reshape(tok_rows, 2, feature_width)
    input_pairs = contract_rows(pair_place, back_input).reshape(tok_rows, 2, feature_width)
    mixture = jnp.sum(gate_share[:, :, None] * out_pairs, axis=1)
    mixed = (tok_float + mixture).astype(jnp.bfloat16)
    normed_grad = jnp.sum(input_pairs, axis=1)
    gain_grad = lax.psum(jnp.sum(normed_grad * tok_float * inv_rms, axis=0), ("dp", "expert"))
    scaled = normed_grad * norm_gain[None, :]
    inner_mean = jnp.mean(scaled * tok_float, axis=1, keepdims=True)
    tokens_grad = (
        out_grad.astype(jnp.float32)
        + inv_rms * scaled
        - inv_rms * inv_rms * inv_rms * tok_float * inner_mean
    ).astype(jnp.bfloat16)
    hidden_rows = gate_own.shape[0]
    w_gate_grad = gradients[:, :feature_width].reshape(1, hidden_rows, feature_width)
    w_up_grad = gradients[:, feature_width : 2 * feature_width].reshape(
        1, hidden_rows, feature_width
    )
    w_down_grad = gradients[:, 2 * feature_width :].reshape(1, hidden_rows, feature_width)
    return (mixed, tokens_grad, gain_grad, w_gate_grad, w_up_grad, w_down_grad)


def solution(mesh):
    in_specs = (
        P(("dp", "expert"), None),
        P(),
        P(("dp", "expert"), None),
        P(("dp", "expert"), None),
        P("expert", "dp", None),
        P("expert", "dp", None),
        P("expert", "dp", None),
        P(("dp", "expert"), None),
    )
    out_specs = (
        P(("dp", "expert"), None),
        P(("dp", "expert"), None),
        P(),
        P("expert", "dp", None),
        P("expert", "dp", None),
        P("expert", "dp", None),
    )
    return jax.shard_map(
        on_device, mesh=mesh, in_specs=in_specs, out_specs=out_specs, check_vma=False
    )
```

profile of v0, /device:TPU:0, one launch (start us, length us, event | category | flops | bytes accessed | tf_op | source)
XLA Modules:
  0.0 279.3 jit_solution(15544802298158846418)
XLA Ops:
  7.2 0.0 copy-start.1
  7.2 0.0 all-gather.11.cloned.1.call-start
  7.2 0.7 all-gather.11.cloned.1.call-update
  7.9 0.0 all-gather.9.cloned.1.call-start
  8.0 0.7 all-gather.9.cloned.1.call-update
  8.7 0.0 all-gather.7.cloned.1.call-start
  8.7 0.7 all-gather.7.cloned.1.call-update
  9.4 0.0 copy-done.4
  9.4 0.1 copy.39
  9.5 0.1 eq.65
  9.7 0.1 reshape.131
  9.8 0.0 copy-start.5
  9.9 0.4 mul.156
  10.3 1.1 mul.157
  11.4 0.1 copy.43
  11.5 0.1 mul.154
  11.7 0.9 reduce-window.6
  12.5 0.2 slice_reduce_fusion
  12.8 0.1 fusion.37
  12.9 0.0 copy-start
  12.9 0.0 copy-start.3
  12.9 1.9 convolution_convert_fusion.3
  14.8 7.3 %all-to-all-start.2 = ((bf16[8,72,1024]{2,1,0:T(8,128)(2,1)}), bf16[8,72,1024]{2,1,0:T(8,128)(2,1)S(1)}, u32[]{:S(2)}, u32[]{:S(2)}) async-start(bf16[8,72,1024]{2,1,0:T(8,128)(2,1)} %bitcast.10), calls=%async_computation.2 | async-start | bytes 2359296 | tf_op jit(solution)/shard_map/all_to_all | solution.py:76
  22.1 0.1 reduce_sum.57
  22.2 0.1 copy.41
  22.3 0.2 fusion.18
  22.5 0.2 fusion.19
  22.7 1.6 convolution_convert_fusion.4
  24.3 26.4 %all-to-all-done.2 = bf16[8,72,1024]{2,1,0:T(8,128)(2,1)S(1)} async-done(((bf16[8,72,1024]{2,1,0:T(8,128)(2,1)}), bf16[8,72,1024]{2,1,0:T(8,128)(2,1)S(1)}, u32[]{:S(2)}, u32[]{:S(2)}) %all-to-all-start.2) | async-done | bytes 1179680 | tf_op jit(solution)/shard_map/all_to_all | solution.py:76
  50.7 3.6 %all-to-all-start = ((bf16[8,72,1024]{2,1,0:T(8,128)(2,1)}), bf16[8,72,1024]{2,1,0:T(8,128)(2,1)S(1)}, u32[]{:S(2)}, u32[]{:S(2)}) async-start(bf16[8,72,1024]{2,1,0:T(8,128)(2,1)} %bitcast.2), calls=%async_computation | async-start | bytes 2359296 | tf_op jit(solution)/shard_map/all_to_all | solution.py:75
  54.3 0.2 reduce-scatter.2.cloned.1.call-start
  54.5 0.0 all-gather.11.cloned.1.call-done
  54.6 6.9 %fusion.1 = f32[576,2048]{1,0:T(8,128)} fusion(bf16[576,1024]{1,0:T(8,128)(2,1)S(1)} %bitcast.63, bf16[1,2048,1024]{2,1,0:T(8,128)(2,1)} %all-gather.11.cloned.1.call-done), kind=kOutput, calls=%fused_computation.6 | convolution fusion | flops 2415919104 | bytes 10092544 | tf_op jit(solution)/shard_map/dot_general | solution.py:29
  61.5 21.6 %all-to-all-done = bf16[8,72,1024]{2,1,0:T(8,128)(2,1)S(1)} async-done(((bf16[8,72,1024]{2,1,0:T(8,128)(2,1)}), bf16[8,72,1024]{2,1,0:T(8,128)(2,1)S(1)}, u32[]{:S(2)}, u32[]{:S(2)}) %all-to-all-start) | async-done | bytes 1179680 | tf_op jit(solution)/shard_map/all_to_all | solution.py:75
  83.1 6.5 %fusion.7 = f32[576,2048]{1,0:T(8,128)} fusion(bf16[576,1024]{1,0:T(8,128)(2,1)S(1)} %bitcast.65, bf16[1,2048,1024]{2,1,0:T(8,128)(2,1)} %all-gather.9.cloned.1.call-done), kind=kOutput, calls=%fused_computation.12 | convolution fusion | flops 2415919104 | bytes 10092544 | tf_op jit(solution)/shard_map/dot_general | solution.py:25
  89.6 29.3 %all-gather.7.cloned.1.call-done = bf16[1,2048,1024]{2,1,0:T(8,128)(2,1)} async-done(((bf16[1,512,1024]{2,1,0:T(8,128)(2,1)}), bf16[1,2048,1024]{2,1,0:T(8,128)(2,1)}) %all-gather.7.cloned.1.call-update) | async-done | bytes 4194320 | tf_op jit(solution)/shard_map/all_gather | solution.py:80
  118.9 8.5 %multiply_convert_fusion.1 = (bf16[576,2048]{1,0:T(8,128)(2,1)S(1)}, bf16[576,2048]{1,0:T(8,128)(2,1)S(1)}, bf16[576,2048]{1,0:T(8,128)(2,1)S(1)}) fusion(f32[576,2048]{1,0:T(8,128)} %fusion.1, f32[576,2048]{1,0:T(8,128)} %fusion.7, bf16[576,1024]{1,0:T(8,128)(2,1)S(1)} %bitcast.66, bf16[1,2048,1024]{2,1,0:T(8,128)(2,1)} %all-gather.7.cloned.1.call-done), kind=kOutput, calls=%fused_computation.2 | convolution fusion | flops 2433613824 | bytes 21889024 | tf_op jit(solution)/shard_map/dot_general | solution.py:22
  127.4 0.0 copy-start.9
  127.4 0.0 copy-start.10
  127.4 3.8 %convolution_convert_fusion = bf16[2048,1024]{0,1:T(8,128)(2,1)S(1)} fusion(bf16[576,2048]{1,0:T(8,128)(2,1)S(1)} %get-tuple-element.34, bf16[576,1024]{1,0:T(8,128)(2,1)S(1)} %bitcast.64), kind=kOutput, calls=%fused_computation.18 | convolution fusion | flops 2418016256 | bytes 7733248 | tf_op jit(solution)/shard_map/dot_general | solution.py:48
  131.2 3.8 %convolution_convert_fusion.1 = bf16[2048,1024]{0,1:T(8,128)(2,1)S(1)} fusion(bf16[576,2048]{1,0:T(8,128)(2,1)S(1)} %get-tuple-element.33, bf16[576,1024]{1,0:T(8,128)(2,1)S(1)} %bitcast.67), kind=kOutput, calls=%fused_computation.19 | convolution fusion | flops 2418016256 | bytes 7733248 | tf_op jit(solution)/shard_map/dot_general | solution.py:48
  135.0 3.8 %convolution_convert_fusion.2 = bf16[2048,1024]{0,1:T(8,128)(2,1)S(1)} fusion(bf16[576,2048]{1,0:T(8,128)(2,1)S(1)} %get-tuple-element.32, bf16[576,1024]{1,0:T(8,128)(2,1)S(1)} %bitcast.68), kind=kOutput, calls=%fused_computation.20 | convolution fusion | flops 2418016256 | bytes 7733248 | tf_op jit(solution)/shard_map/dot_general | solution.py:48
  138.9 21.6 %pad_maximum_fusion = bf16[2048,3072]{0,1:T(8,128)(2,1)} fusion(bf16[2048,1024]{0,1:T(8,128)(2,1)S(1)} %convolution_convert_fusion, bf16[2048,1024]{0,1:T(8,128)(2,1)S(1)} %convolution_convert_fusion.1, bf16[2048,1024]{0,1:T(8,128)(2,1)S(1)} %convolution_convert_fusion.2), kind=kLoop, calls=%fused_computation | loop fusion | flops 37748736 | bytes 25165824 | tf_op jit(solution)/shard_map/concatenate | solution.py:89
  160.4 0.0 reduce-scatter.2.cloned.1.call-update
  160.5 5.2 %fusion.5 = f32[576,1024]{1,0:T(8,128)S(1)} fusion(bf16[576,2048]{1,0:T(8,128)(2,1)} %copy-done.10, bf16[1,2048,1024]{2,1,0:T(8,128)(2,1)} %all-gather.9.cloned.1.call-done), kind=kOutput, calls=%fused_computation.10 | convolution fusion | flops 2415919104 | bytes 8912896 | tf_op jit(solution)/shard_map/dot_general | solution.py:41
  165.7 3.7 %add_convert_fusion = bf16[576,1024]{1,0:T(8,128)(2,1)} fusion(f32[576,1024]{1,0:T(8,128)S(1)} %fusion.5, bf16[576,2048]{1,0:T(8,128)(2,1)S(1)} %copy-done.8, bf16[1,2048,1024]{2,1,0:T(8,128)(2,1)S(1)} %copy-done.6), kind=kOutput, calls=%fused_computation.21 | convolution fusion | flops 2417098752 | bytes 10092544 | tf_op jit(solution)/shard_map/dot_general | solution.py:41
  169.4 5.5 %all-to-all-start.3 = ((bf16[8,72,1024]{2,1,0:T(8,128)(2,1)}), bf16[8,72,1024]{2,1,0:T(8,128)(2,1)S(1)}, u32[]{:S(2)}, u32[]{:S(2)}) async-start(bf16[8,72,1024]{2,1,0:T(8,128)(2,1)} %bitcast.12), calls=%async_computation.3 | async-start | bytes 2359296 | tf_op jit(solution)/shard_map/all_to_all | solution.py:103
  174.9 7.7 %fusion.15 = bf16[576,1024]{1,0:T(8,128)(2,1)} fusion(bf16[576,2048]{1,0:T(8,128)(2,1)} %copy-done.9, bf16[1,2048,1024]{2,1,0:T(8,128)(2,1)} %all-gather.11.cloned.1.call-done), kind=kOutput, calls=%fused_computation.34 | convolution fusion | flops 2416508928 | bytes 7733248 | tf_op jit(solution)/shard_map/dot_general | solution.py:40
  182.6 21.3 %all-to-all-done.3 = bf16[8,72,1024]{2,1,0:T(8,128)(2,1)S(1)} async-done(((bf16[8,72,1024]{2,1,0:T(8,128)(2,1)}), bf16[8,72,1024]{2,1,0:T(8,128)(2,1)S(1)}, u32[]{:S(2)}, u32[]{:S(2)}) %all-to-all-start.3) | async-done | bytes 1179680 | tf_op jit(solution)/shard_map/all_to_all | solution.py:103
  203.9 3.6 %all-to-all-start.1 = ((bf16[8,72,1024]{2,1,0:T(8,128)(2,1)}), bf16[8,72,1024]{2,1,0:T(8,128)(2,1)S(1)}, u32[]{:S(2)}, u32[]{:S(2)}) async-start(bf16[8,72,1024]{2,1,0:T(8,128)(2,1)} %bitcast.7), calls=%async_computation.1 | async-start | bytes 2359296 | tf_op jit(solution)/shard_map/all_to_all | solution.py:102
  207.5 0.2 iota_compare_fusion.1
  207.8 1.0 eq.71
  208.8 1.9 convolution_reduce_fusion
  210.7 0.0 copy-start.2
  210.7 0.3 fusion.28
  211.0 45.6 %psum.7 = f32[1024]{0:T(1024)} all-reduce(f32[1024]{0:T(1024)S(1)} %get-tuple-element.30), channel_id=1, replica_groups=mesh['dp'=4,'expert'=8] {'dp','expert'}, use_global_device_ids=true, to_apply=%region_9.10 | all-reduce | flops 1024 | bytes 8192 | tf_op jit(solution)/shard_map/psum | solution.py:110
  256.5 0.0 all-to-all-done.1
  256.5 1.9 multiply_reduce_fusion
  258.5 1.2 fusion.25
  259.7 2.8 convert_element_type.69
  262.5 2.7 slice_bitcast_fusion
  265.2 2.9 %copy.45 = f32[1,512,1024]{2,1,0:T(8,128)} copy(f32[1,512,1024]{1,2,0:T(8,128)} %get-tuple-element.37) | data formatting | bytes 4194304
  268.1 2.9 %copy.46 = f32[1,512,1024]{2,1,0:T(8,128)} copy(f32[1,512,1024]{1,2,0:T(8,128)} %get-tuple-element.36) | data formatting | bytes 4194304
  271.0 1.8 copy.47
  (22 shorter events, 0.1 us)
Async XLA Ops:
  7.2 2.2 copy-start.4
  7.2 2.7 copy-start.1
  7.2 47.4 %all-gather.11.cloned.1.call-start = ((), (), s32[]{:S(2)}) async-start(), calls=%async_computation.8 | async-start | bytes 5242880 | tf_op jit(solution)/shard_map/all_gather | solution.py:82
  7.9 75.1 %all-gather.9.cloned.1.call-start = ((), (), s32[]{:S(2)}) async-start(), calls=%async_computation.7 | async-start | bytes 5242880 | tf_op jit(solution)/shard_map/all_gather | solution.py:81
  8.7 110.2 %all-gather.7.cloned.1.call-start = ((), (), s32[]{:S(2)}) async-start(), calls=%async_computation.6 | async-start | bytes 5242880 | tf_op jit(solution)/shard_map/all_gather | solution.py:80
  9.8 1.5 copy-start.5
  12.9 9.6 %copy-start = (bf16[192,1024]{1,0:T(8,128)(2,1)S(1)}, bf16[192,1024]{1,0:T(8,128)(2,1)}, u32[]{:S(2)}) copy-start(bf16[192,1024]{1,0:T(8,128)(2,1)} %param.8) | copy-start | bytes 1179652
  12.9 9.8 %copy-start.3 = (f32[1024]{0:T(1024)S(1)}, f32[1024]{0:T(1024)}, u32[]{:S(2)}) copy-start(f32[1024]{0:T(1024)} %param.9) | copy-start | bytes 12292
  14.8 35.9 %all-to-all-start.2 = ((bf16[8,72,1024]{2,1,0:T(8,128)(2,1)}), bf16[8,72,1024]{2,1,0:T(8,128)(2,1)S(1)}, u32[]{:S(2)}, u32[]{:S(2)}) async-start(bf16[8,72,1024]{2,1,0:T(8,128)(2,1)} %bitcast.10), calls=%async_computation.2 | async-start | bytes 2359296 | tf_op jit(solution)/shard_map/all_to_all | solution.py:76
  50.7 32.4 %all-to-all-start = ((bf16[8,72,1024]{2,1,0:T(8,128)(2,1)}), bf16[8,72,1024]{2,1,0:T(8,128)(2,1)S(1)}, u32[]{:S(2)}, u32[]{:S(2)}) async-start(bf16[8,72,1024]{2,1,0:T(8,128)(2,1)} %bitcast.2), calls=%async_computation | async-start | bytes 2359296 | tf_op jit(solution)/shard_map/all_to_all | solution.py:75
  54.3 205.4 %reduce-scatter.2.cloned.1.call-start = ((), (), s32[]{:S(2)}) async-start(), calls=%async_computation.5 | async-start | bytes 15728640 | tf_op jit(solution)/shard_map/reduce_scatter | solution.py:88
  127.4 3.8 %copy-start.9 = (bf16[576,2048]{1,0:T(8,128)(2,1)}, bf16[576,2048]{1,0:T(8,128)(2,1)S(1)}, u32[]{:S(2)}) copy-start(bf16[576,2048]{1,0:T(8,128)(2,1)S(1)} %get-tuple-element.34) | copy-start | bytes 7077892
  127.4 3.8 %copy-start.10 = (bf16[576,2048]{1,0:T(8,128)(2,1)}, bf16[576,2048]{1,0:T(8,128)(2,1)S(1)}, u32[]{:S(2)}) copy-start(bf16[576,2048]{1,0:T(8,128)(2,1)S(1)} %get-tuple-element.33) | copy-start | bytes 7077892
  127.4 7.7 %copy-start.7 = (bf16[576,2048]{1,0:T(8,128)(2,1)}, bf16[576,2048]{1,0:T(8,128)(2,1)S(1)}, u32[]{:S(2)}) copy-start(bf16[576,2048]{1,0:T(8,128)(2,1)S(1)} %get-tuple-element.32) | copy-start | bytes 7077892
  160.4 5.3 %copy-start.6 = (bf16[1,2048,1024]{2,1,0:T(8,128)(2,1)S(1)}, bf16[1,2048,1024]{2,1,0:T(8,128)(2,1)}, u32[]{:S(2)}) copy-start(bf16[1,2048,1024]{2,1,0:T(8,128)(2,1)} %all-gather.7.cloned.1.call-done) | copy-start | bytes 12582916
  160.4 5.3 %copy-start.8 = (bf16[576,2048]{1,0:T(8,128)(2,1)S(1)}, bf16[576,2048]{1,0:T(8,128)(2,1)}, u32[]{:S(2)}) copy-start(bf16[576,2048]{1,0:T(8,128)(2,1)} %copy-done.7) | copy-start | bytes 7077892
  169.4 34.5 %all-to-all-start.3 = ((bf16[8,72,1024]{2,1,0:T(8,128)(2,1)}), bf16[8,72,1024]{2,1,0:T(8,128)(2,1)S(1)}, u32[]{:S(2)}, u32[]{:S(2)}) async-start(bf16[8,72,1024]{2,1,0:T(8,128)(2,1)} %bitcast.12), calls=%async_computation.3 | async-start | bytes 2359296 | tf_op jit(solution)/shard_map/all_to_all | solution.py:103
  203.9 52.6 %all-to-all-start.1 = ((bf16[8,72,1024]{2,1,0:T(8,128)(2,1)}), bf16[8,72,1024]{2,1,0:T(8,128)(2,1)S(1)}, u32[]{:S(2)}, u32[]{:S(2)}) async-start(bf16[8,72,1024]{2,1,0:T(8,128)(2,1)} %bitcast.7), calls=%async_computation.1 | async-start | bytes 2359296 | tf_op jit(solution)/shard_map/all_to_all | solution.py:102
  210.7 47.8 %copy-start.2 = (bf16[192,1024]{1,0:T(8,128)(2,1)S(1)}, bf16[192,1024]{1,0:T(8,128)(2,1)}, u32[]{:S(2)}) copy-start(bf16[192,1024]{1,0:T(8,128)(2,1)} %param.15) | copy-start | bytes 1179652
Sparse Core Ops, SparseCore 0:
  9.6 37.1 all-gather.10
  48.3 34.4 all-gather.8
  84.4 34.4 all-gather.6
  160.6 98.5 reduce-scatter.1
where the time goes:
time: 280 us; the launch traced here: 279 us
  waiting for transfers between devices  101 us (36%)
  matrix products  57.2 us (20%)
  blocking collectives  45.6 us (16%)
  other arithmetic  27.4 us (10%)
  starting transfers between devices  20.4 us (7%)
  between operations  14.1 us (5%)
  local copies, waits for them, and re-layouts  14 us (5%)
    psum x1, blocking collectives, on_device(): lax.psum(jnp.sum(normed_grad * tok_float * inv_rms, axis=0), ('dp', 'expe...  45.6 us
    all_gather x1, waiting for transfers between devices, on_device(): lax.all_gather(gate_own, 'dp', axis=0, tiled=True)  29.3 us
    all_to_all x1, waiting for transfers between devices, on_device(): lax.all_to_all(send_cot, 'expert', split_axis=0, concat_axis=0, tiled=True)  26.4 us
    all_to_all x1, waiting for transfers between devices, on_device(): lax.all_to_all(send_rows, 'expert', split_axis=0, concat_axis=0, tiled=True)  21.6 us
    concatenate x1, other arithmetic, on_device(): jnp.concatenate([contract_rows(gate_grad, in_rows), contract_rows(up_grad...  21.6 us
    all_to_all x1, waiting for transfers between devices, on_device(): lax.all_to_all(input_rows, 'expert', split_axis=0, concat_axis=0, tiled=T...  21.3 us
    dot_general x5, matrix products, contract_rows(): lax.dot_general(left, right, contract_first, preferred_element_type=jnp.f...  15.2 us
    dot_general x1, matrix products, expert_inner(): lax.dot_general(in_rows, gate_weight, contract_last, preferred_element_ty...  8.48 us
  transfers between devices with their start and end apart: 8, of which 4 were waited for; matrix products, arithmetic and copies ran while one was open for 16% of the time, Pallas kernels for 0%

commit v1 on v0

--- a/solution.py
+++ b/solution.py
@@ -48,7 +48,18 @@
     return lax.dot_general(left, right, contract_first, preferred_element_type=jnp.float32)
 
 
-def on_device(tokens, norm_gain, expert_ids, gate_share, w_gate, w_up, w_down, out_grad):
+def sum_all(value, axes):
+    total = value.reshape(8, -1)
+    for axis in axes:
+        size, step = lax.axis_size(axis), 1
+        assert size & (size - 1) == 0
+        while step < size:
+            total = total + lax.ppermute(total, axis, [(i, i ^ step) for i in range(size)])
+            step *= 2
+    return total.reshape(value.shape)
+
+
+def layer_step(tokens, norm_gain, expert_ids, gate_share, w_gate, w_up, w_down, out_grad):
     tok_rows, feature_width = tokens.shape
     experts_n = lax.axis_size("expert")
     capacity = 3 * tok_rows // experts_n
@@ -71,43 +82,65 @@
     send_cot = jnp.dot(pair_place, pair_cot, preferred_element_type=jnp.float32).astype(
         jnp.bfloat16
     )
-    in_rows, cot_rows = (
-        lax.all_to_all(send_rows, "expert", split_axis=0, concat_axis=0, tiled=True),
-        lax.all_to_all(send_cot, "expert", split_axis=0, concat_axis=0, tiled=True),
+    in_rows = lax.all_to_all(send_rows, "expert", split_axis=0, concat_axis=0, tiled=True)
+    cot_rows = lax.all_to_all(send_cot, "expert", split_axis=0, concat_axis=0, tiled=True)
+    gate_own, up_own, down_own = (w_gate[0], w_up[0], w_down[0])
+    across = [(i, i ^ 2) for i in range(lax.axis_size("dp"))]
+    beside = [(i, i ^ 1) for i in range(lax.axis_size("dp"))]
+
+    def far(value):
+        return lax.ppermute(value, "dp", across)
+
+    def near(value):
+        return lax.ppermute(value, "dp", beside)
+
+    gate_far = far(gate_own)
+    up_far = far(up_own)
+    down_far = far(down_own)
+    local = [jnp.concatenate([own, near(own)], axis=0) for own in (gate_own, up_own, down_own)]
+    diagonals = [near(value) for value in (gate_far, up_far, down_far)]
+    remote = [
+        jnp.concatenate(pair, axis=0) for pair in zip((gate_far, up_far, down_far), diagonals)
+    ]
+    own_units = gate_own.shape[0]
+    remote_block = expert_inner(in_rows, cot_rows, *remote)
+    local_block = expert_inner(in_rows, cot_rows, *local)
+
+    def partials(block):
+        hidden, gate_grad, up_grad = block
+        return [
+            contract_rows(left, right).astype(jnp.bfloat16)
+            for left, right in ((hidden, cot_rows), (gate_grad, in_rows), (up_grad, in_rows))
+        ]
+
+    summed = []
+    for product in partials(remote_block):
+        other = near(product[own_units:]).astype(jnp.float32)
+        summed.append((product[:own_units].astype(jnp.float32) + other).astype(jnp.bfloat16))
+    arrived = [far(summed[0])]
+    arrived.append(far(summed[1]))
+    arrived.append(far(summed[2]))
+    local_products = partials(local_block)
+    w_down_grad, w_gate_grad, w_up_grad = (
+        (
+            product[:own_units].astype(jnp.float32)
+            + near(product[own_units:]).astype(jnp.float32)
+            + landed.astype(jnp.float32)
+        )[None]
+        for product, landed in zip(local_products, arrived)
     )
-    gate_own, up_own, down_own = (w_gate[0], w_up[0], w_down[0])
-    gate_all, up_all, down_all = (
-        lax.all_gather(gate_own, "dp", axis=0, tiled=True),
-        lax.all_gather(up_own, "dp", axis=0, tiled=True),
-        lax.all_gather(down_own, "dp", axis=0, tiled=True),
-    )
-    hidden, gate_grad, up_grad = expert_inner(in_rows, cot_rows, gate_all, up_all, down_all)
-    out_part, input_part = expert_outer(hidden, gate_grad, up_grad, gate_all, up_all, down_all)
-    out_rows = out_part.astype(jnp.bfloat16)
-    input_rows = input_part.astype(jnp.bfloat16)
-    gradients = lax.psum_scatter(
-        jnp.concatenate(
-            [
-                contract_rows(gate_grad, in_rows),
-                contract_rows(up_grad, in_rows),
-                contract_rows(hidden, cot_rows),
-            ],
-            axis=1,
-        ).astype(jnp.bfloat16),
-        "dp",
-        scatter_dimension=0,
-        tiled=True,
-    ).astype(jnp.float32)
-    back_out, back_input = (
-        lax.all_to_all(out_rows, "expert", split_axis=0, concat_axis=0, tiled=True),
-        lax.all_to_all(input_rows, "expert", split_axis=0, concat_axis=0, tiled=True),
-    )
+    remote_out, remote_input = expert_outer(*remote_block, *remote)
+    local_out, local_input = expert_outer(*local_block, *local)
+    out_rows = (remote_out + local_out).astype(jnp.bfloat16)
+    input_rows = (remote_input + local_input).astype(jnp.bfloat16)
+    back_input = lax.all_to_all(input_rows, "expert", split_axis=0, concat_axis=0, tiled=True)
+    back_out = lax.all_to_all(out_rows, "expert", split_axis=0, concat_axis=0, tiled=True)
     out_pairs = contract_rows(pair_place, back_out).reshape(tok_rows, 2, feature_width)
     input_pairs = contract_rows(pair_place, back_input).reshape(tok_rows, 2, feature_width)
     mixture = jnp.sum(gate_share[:, :, None] * out_pairs, axis=1)
     mixed = (tok_float + mixture).astype(jnp.bfloat16)
     normed_grad = jnp.sum(input_pairs, axis=1)
-    gain_grad = lax.psum(jnp.sum(normed_grad * tok_float * inv_rms, axis=0), ("dp", "expert"))
+    gain_grad = sum_all(jnp.sum(normed_grad * tok_float * inv_rms, axis=0), ("expert", "dp"))
     scaled = normed_grad * norm_gain[None, :]
     inner_mean = jnp.mean(scaled * tok_float, axis=1, keepdims=True)
     tokens_grad = (
@@ -115,12 +148,6 @@
         + inv_rms * scaled
         - inv_rms * inv_rms * inv_rms * tok_float * inner_mean
     ).astype(jnp.bfloat16)
-    hidden_rows = gate_own.shape[0]
-    w_gate_grad = gradients[:, :feature_width].reshape(1, hidden_rows, feature_width)
-    w_up_grad = gradients[:, feature_width : 2 * feature_width].reshape(
-        1, hidden_rows, feature_width
-    )
-    w_down_grad = gradients[:, 2 * feature_width :].reshape(1, hidden_rows, feature_width)
     return (mixed, tokens_grad, gain_grad, w_gate_grad, w_up_grad, w_down_grad)
 
 
@@ -144,5 +171,5 @@
         P("expert", "dp", None),
     )
     return jax.shard_map(
-        on_device, mesh=mesh, in_specs=in_specs, out_specs=out_specs, check_vma=False
+        layer_step, mesh=mesh, in_specs=in_specs, out_specs=out_specs, check_vma=False
     )

time: 280 us -> 271 us (0.968); the launches traced: 279 us -> 266 us
  blocking collectives: 45.6 us -> 0 us
  starting transfers between devices: 20.4 us -> 41 us
  between operations: 14.1 us -> 1.44 us
  matrix products: 57.2 us -> 69.3 us
  local copies, waits for them, and re-layouts: 14 us -> 25.5 us
  other arithmetic: 27.4 us -> 21 us
  waiting for transfers between devices: 101 us -> 107 us
    ppermute x0 -> x23, waiting for transfers between devices: none -> 81.8 us  [the longest x6 51.8 us: far(): return lax.ppermute(value, 'dp', across)]
    psum x1 -> x0, blocking collectives: 45.6 us -> none  [on_device(): lax.psum(jnp.sum(normed_grad * tok_float * inv_rms, axis=0), ('dp', 'expe...]
    all_to_all x4, waiting for transfers between devices: 69.3 us -> 25.6 us  [the longest x1 23.4 us: layer_step(): lax.all_to_all(send_rows, 'expert', split_axis=0, concat_axis=0, tiled=True)]
    all_gather x3 -> x0, waiting for transfers between devices: 29.3 us -> none  [the longest x1 29.3 us: on_device(): lax.all_gather(gate_own, 'dp', axis=0, tiled=True)]
    concatenate x1 -> x0, other arithmetic: 21.6 us -> none  [on_device(): jnp.concatenate([contract_rows(gate_grad, in_rows), contract_rows(up_grad...]
    ppermute x0 -> x23, starting transfers between devices: none -> 19.7 us  [the longest x5 9.61 us: sum_all(): lax.ppermute(total, axis, [(i, i ^ step) for i in range(size)])]
    broadcast_in_dim x0 -> x3, other arithmetic: none -> 9.1 us  [layer_step(): (product[:own_units].astype(jnp.float32) + near(product[own_units:]).asty...]
    dot_general x5 -> x8, matrix products: 15.2 us -> 23.8 us  [contract_rows(): lax.dot_general(left, right, contract_first, preferred_element_type=jnp.f...]
  transfers between devices with their start and end apart: 8 -> 27, of which waited for: 4 -> 8; matrix products, arithmetic and copies ran while one was open for 16% -> 34% of each run, Pallas kernels for 0% -> 0%
where the time goes in v1:
time: 271 us; the launch traced here: 266 us
  waiting for transfers between devices  107 us (39%)
  matrix products  69.3 us (26%)
  starting transfers between devices  41 us (15%)
  local copies, waits for them, and re-layouts  25.5 us (9%)
  other arithmetic  21 us (8%)
    ppermute x6, waiting for transfers between devices, far(): return lax.ppermute(value, 'dp', across)  51.8 us
    ppermute x5, waiting for transfers between devices, sum_all(): lax.ppermute(total, axis, [(i, i ^ step) for i in range(size)])  29.9 us
    dot_general x8, matrix products, contract_rows(): lax.dot_general(left, right, contract_first, preferred_element_type=jnp.f...  23.8 us
    all_to_all x1, waiting for transfers between devices, layer_step(): lax.all_to_all(send_rows, 'expert', split_axis=0, concat_axis=0, tiled=True)  23.4 us
    unnamed x67, local copies, waits for them, and re-layouts  11.9 us
    dot_general x2, matrix products, expert_inner(): lax.dot_general(in_rows, gate_weight, contract_last, preferred_element_ty...  9.63 us
    ppermute x5, starting transfers between devices, sum_all(): lax.ppermute(total, axis, [(i, i ^ step) for i in range(size)])  9.61 us
    broadcast_in_dim x3, other arithmetic, layer_step(): (product[:own_units].astype(jnp.float32) + near(product[own_units:]).asty...  9.1 us
  transfers between devices with their start and end apart: 27, of which 8 were waited for; matrix products, arithmetic and copies ran while one was open for 34% of the time, Pallas kernels for 0%

profile of v1, /device:TPU:0, one launch (start us, length us, event | category | flops | bytes accessed | tf_op | source)
XLA Modules:
  0.0 265.6 jit_solution(5075633026315902134)
XLA Ops:
  4.0 1.2 fusion.9
  5.2 2.6 convolution_convert_fusion.7
  7.9 7.3 %all-to-all-start = ((bf16[8,72,1024]{2,1,0:T(8,128)(2,1)}), bf16[8,72,1024]{2,1,0:T(8,128)(2,1)}, u32[]{:S(2)}, u32[]{:S(2)}) async-start(bf16[8,72,1024]{2,1,0:T(8,128)(2,1)} %bitcast.2), calls=%async_computation | async-start | bytes 2359296 | tf_op jit(solution)/shard_map/all_to_all | solution.py:85
  15.2 1.6 collective-permute-start.4
  17.1 1.1 mul.180
  18.5 1.9 convolution_convert_fusion.6
  20.4 23.4 %all-to-all-done = bf16[8,72,1024]{2,1,0:T(8,128)(2,1)} async-done(((bf16[8,72,1024]{2,1,0:T(8,128)(2,1)}), bf16[8,72,1024]{2,1,0:T(8,128)(2,1)}, u32[]{:S(2)}, u32[]{:S(2)}) %all-to-all-start) | async-done | bytes 1179680 | tf_op jit(solution)/shard_map/all_to_all | solution.py:85
  43.8 3.6 %all-to-all-start.2 = ((bf16[8,72,1024]{2,1,0:T(8,128)(2,1)}), bf16[8,72,1024]{2,1,0:T(8,128)(2,1)S(1)}, u32[]{:S(2)}, u32[]{:S(2)}) async-start(bf16[8,72,1024]{2,1,0:T(8,128)(2,1)} %bitcast.10), calls=%async_computation.2 | async-start | bytes 2359296 | tf_op jit(solution)/shard_map/all_to_all | solution.py:86
  47.5 1.5 collective-permute-start.2
  50.3 1.5 eq.71
  51.8 2.3 constant_dynamic-update-slice_fusion.5
  54.1 19.8 %collective-permute-done.2 = bf16[512,1024]{1,0:T(8,128)(2,1)} collective-permute-done((bf16[512,1024]{1,0:T(8,128)(2,1)}, bf16[512,1024]{1,0:T(8,128)(2,1)}, u32[]{:S(2)}, u32[]{:S(2)}) %collective-permute-start.2) | collective-permute-done | bytes 1048608 | tf_op jit(solution)/shard_map/ppermute | solution.py:92
  73.9 2.3 constant_dynamic-update-slice_fusion.3
  76.1 18.9 %collective-permute-done = bf16[512,1024]{1,0:T(8,128)(2,1)} collective-permute-done((bf16[512,1024]{1,0:T(8,128)(2,1)}, bf16[512,1024]{1,0:T(8,128)(2,1)}, u32[]{:S(2)}, u32[]{:S(2)}) %collective-permute-start) | collective-permute-done | bytes 1048608 | tf_op jit(solution)/shard_map/ppermute | solution.py:92
  95.1 1.3 constant_dynamic-update-slice_fusion.1
  97.0 4.7 %fusion.7 = f32[576,1024]{1,0:T(8,128)} fusion(bf16[576,1024]{1,0:T(8,128)(2,1)} %bitcast.3, bf16[512,1024]{1,0:T(8,128)(2,1)} %collective-permute-done.6, bf16[512,1024]{1,0:T(8,128)(2,1)} %bitcast.4), kind=kOutput, calls=%fused_computation.43 | convolution fusion | flops 1212153856 | bytes 5636096 | tf_op jit(solution)/shard_map/dot_general | solution.py:22
  101.7 4.7 %fusion.5 = f32[576,1024]{1,0:T(8,128)} fusion(bf16[576,1024]{1,0:T(8,128)(2,1)} %bitcast.3, bf16[512,1024]{1,0:T(8,128)(2,1)} %collective-permute-done.7, bf16[512,1024]{1,0:T(8,128)(2,1)} %bitcast.5), kind=kOutput, calls=%fused_computation.41 | convolution fusion | flops 1212153856 | bytes 5636096 | tf_op jit(solution)/shard_map/dot_general | solution.py:25
  106.4 6.7 %multiply_convert_fusion = (bf16[576,1024]{1,0:T(8,128)(2,1)S(1)}, bf16[576,1024]{1,0:T(8,128)(2,1)S(1)}, bf16[576,1024]{1,0:T(8,128)(2,1)}) fusion(f32[576,1024]{1,0:T(8,128)} %fusion.7, f32[576,1024]{1,0:T(8,128)} %fusion.5, bf16[576,1024]{1,0:T(8,128)(2,1)S(1)} %bitcast.69, bf16[512,1024]{1,0:T(8,128)(2,1)} %collective-permute-done.8, ...), kind=kOutput, calls=%fused_computation.1 | convolution fusion | flops 1221001216 | bytes 11534336 | tf_op jit(solution)/shard_map/dot_general | solution.py:29
  113.1 3.3 %fusion.6 = f32[576,1024]{1,0:T(8,128)S(1)} fusion(bf16[576,1024]{1,0:T(8,128)(2,1)S(1)} %get-tuple-element.12, bf16[512,1024]{1,0:T(8,128)(2,1)} %collective-permute-done.6, bf16[512,1024]{1,0:T(8,128)(2,1)} %bitcast.4), kind=kOutput, calls=%fused_computation.42 | convolution fusion | flops 1212153856 | bytes 5636096 | tf_op jit(solution)/shard_map/dot_general | solution.py:41
  116.5 2.9 %fusion.4 = f32[576,1024]{1,0:T(8,128)S(1)} fusion(bf16[576,1024]{1,0:T(8,128)(2,1)S(1)} %get-tuple-element.11, bf16[512,1024]{1,0:T(8,128)(2,1)} %collective-permute-done.7, bf16[512,1024]{1,0:T(8,128)(2,1)} %bitcast.5), kind=kOutput, calls=%fused_computation.40 | convolution fusion | flops 1212153856 | bytes 5636096 | tf_op jit(solution)/shard_map/dot_general | solution.py:41
  119.5 4.6 %convolution_convert_fusion.5 = bf16[1024,1024]{1,0:T(8,128)(2,1)} fusion(bf16[576,1024]{1,0:T(8,128)(2,1)S(1)} %get-tuple-element.12, bf16[576,1024]{1,0:T(8,128)(2,1)} %bitcast.3), kind=kOutput, calls=%fused_computation.26 | convolution fusion | flops 1209008128 | bytes 4456448 | tf_op jit(solution)/shard_map/dot_general | solution.py:48
  124.0 1.4 constant_dynamic-update-slice_fusion.4
  125.9 1.6 constant_dynamic-update-slice_fusion.2
  127.5 1.4 fusion.36
  129.0 2.7 %fusion.35 = f32[576,1024]{1,0:T(8,128)S(1)} fusion(bf16[576,1024]{1,0:T(8,128)(2,1)} %bitcast.3, bf16[1024,1024]{1,0:T(8,128)(2,1)S(1)} %constant_dynamic-update-slice_fusion.2), kind=kOutput, calls=%fused_computation.90 | convolution fusion | flops 1207959552 | bytes 5636096 | tf_op jit(solution)/shard_map/dot_general | solution.py:25
  131.7 1.3 constant_dynamic-update-slice_fusion
  133.0 4.9 %multiply_convert_fusion.3 = (bf16[576,1024]{1,0:T(8,128)(2,1)S(1)}, bf16[576,1024]{1,0:T(8,128)(2,1)S(1)}, bf16[576,1024]{1,0:T(8,128)(2,1)}) fusion(f32[576,1024]{1,0:T(8,128)S(1)} %fusion.36, f32[576,1024]{1,0:T(8,128)S(1)} %fusion.35, bf16[576,1024]{1,0:T(8,128)(2,1)} %bitcast.3, bf16[1024,1024]{1,0:T(8,128)(2,1)S(1)} %constant_dynamic-update-slice_fusion), kind=kOutput, calls=%fused_computation.4 | convolution fusion | flops 1216806912 | bytes 11534336 | tf_op jit(solution)/shard_map/dot_general | solution.py:22
  137.9 1.4 fusion.37
  139.3 2.7 add_convert_fusion
  142.0 5.9 %all-to-all-start.3 = ((bf16[8,72,1024]{2,1,0:T(8,128)(2,1)}), bf16[8,72,1024]{2,1,0:T(8,128)(2,1)}, u32[]{:S(2)}, u32[]{:S(2)}) async-start(bf16[8,72,1024]{2,1,0:T(8,128)(2,1)} %bitcast.12), calls=%async_computation.3 | async-start | bytes 2359296 | tf_op jit(solution)/shard_map/all_to_all | solution.py:136
  147.8 3.3 %convolution_convert_fusion.3 = bf16[1024,1024]{1,0:T(8,128)(2,1)S(1)} fusion(bf16[576,1024]{1,0:T(8,128)(2,1)S(1)} %copy-done.27, bf16[576,1024]{1,0:T(8,128)(2,1)} %bitcast.3), kind=kOutput, calls=%fused_computation.24 | convolution fusion | flops 1209008128 | bytes 4456448 | tf_op jit(solution)/shard_map/dot_general | solution.py:48
  152.2 1.1 slice.62
  154.3 1.8 convolution_convert_fusion.1
  156.1 1.2 slice.66
  157.3 3.0 %fusion.3 = f32[576,1024]{1,0:T(8,128)S(1)} fusion(bf16[576,1024]{1,0:T(8,128)(2,1)S(1)} %copy-done.25, bf16[512,1024]{1,0:T(8,128)(2,1)} %collective-permute-done.8, bf16[512,1024]{1,0:T(8,128)(2,1)} %bitcast.6), kind=kOutput, calls=%fused_computation.39 | convolution fusion | flops 1212153856 | bytes 5636096 | tf_op jit(solution)/shard_map/dot_general | solution.py:40
  160.3 3.1 %convolution_convert_fusion.4 = bf16[1024,1024]{1,0:T(8,128)(2,1)S(1)} fusion(bf16[576,1024]{1,0:T(8,128)(2,1)S(1)} %copy-done.15, bf16[576,1024]{1,0:T(8,128)(2,1)} %bitcast.3), kind=kOutput, calls=%fused_computation.25 | convolution fusion | flops 1209008128 | bytes 4456448 | tf_op jit(solution)/shard_map/dot_general | solution.py:48
  164.5 1.1 copy-done.30
  165.6 3.2 %convolution_convert_fusion.2 = bf16[1024,1024]{1,0:T(8,128)(2,1)S(1)} fusion(bf16[576,1024]{1,0:T(8,128)(2,1)S(1)} %copy-done.30, bf16[576,1024]{1,0:T(8,128)(2,1)} %bitcast.3), kind=kOutput, calls=%fused_computation.23 | convolution fusion | flops 1209008128 | bytes 4456448 | tf_op jit(solution)/shard_map/dot_general | solution.py:48
  168.9 1.3 copy-done.6
  170.2 1.1 slice.64
  172.1 2.4 add_convert_fusion.1
  174.6 2.1 all-to-all-done.3
  176.7 4.5 %all-to-all-start.1 = ((bf16[8,72,1024]{2,1,0:T(8,128)(2,1)}), bf16[8,72,1024]{2,1,0:T(8,128)(2,1)}, u32[]{:S(2)}, u32[]{:S(2)}) async-start(bf16[8,72,1024]{2,1,0:T(8,128)(2,1)} %bitcast.73), calls=%async_computation.1 | async-start | bytes 2359296 | tf_op jit(solution)/shard_map/all_to_all | solution.py:137
  181.2 3.1 %convolution_convert_fusion = bf16[1024,1024]{1,0:T(8,128)(2,1)S(1)} fusion(bf16[576,1024]{1,0:T(8,128)(2,1)} %get-tuple-element.10, bf16[576,1024]{1,0:T(8,128)(2,1)S(1)} %bitcast.72), kind=kOutput, calls=%fused_computation.21 | convolution fusion | flops 1209008128 | bytes 4456448 | tf_op jit(solution)/shard_map/dot_general | solution.py:48
  185.3 2.2 convolution_reduce_fusion
  187.9 2.0 collective-permute-start.9
  189.9 2.6 add_convert_fusion.4
  192.5 1.5 collective-permute-start.16
  194.0 1.5 collective-permute-start.10
  195.5 2.6 add_convert_fusion.3
  198.1 1.9 collective-permute-done.10
  200.0 1.5 collective-permute-start.19
  201.5 4.6 %collective-permute-start.11 = (f32[8,128]{1,0:T(8,128)S(1)}, f32[8,128]{1,0:T(8,128)S(1)}, u32[]{:S(2)}, u32[]{:S(2)}) collective-permute-start(f32[8,128]{1,0:T(8,128)S(1)} %fusion.71), channel_id=1, source_target_pairs={{0,4},{1,5},{2,6},{3,7},{4,0},{5,1},{6,2},{7,3},{8,12},{9,13},{10,... | collective-permute-start | bytes 12296 | tf_op jit(solution)/shard_map/ppermute | solution.py:57
  206.0 1.4 add_convert_fusion.2
  207.4 2.2 collective-permute-done.11
  209.6 2.4 multiply_reduce_fusion
  212.1 1.6 collective-permute-start.13
  213.9 25.8 %collective-permute-done.13 = f32[8,128]{1,0:T(8,128)S(1)} collective-permute-done((f32[8,128]{1,0:T(8,128)S(1)}, f32[8,128]{1,0:T(8,128)S(1)}, u32[]{:S(2)}, u32[]{:S(2)}) %collective-permute-start.13) | collective-permute-done | bytes 4128 | tf_op jit(solution)/shard_map/ppermute | solution.py:57
  239.8 1.5 collective-permute-start.22
  241.3 1.2 fusion.15
  243.1 3.6 %add_bitcast_fusion.2 = f32[1,512,1024]{2,1,0:T(8,128)} fusion(bf16[512,1024]{1,0:T(8,128)(2,1)} %collective-permute-done.16, bf16[512,1024]{1,0:T(8,128)(2,1)} %collective-permute-done.14, bf16[1024,1024]{1,0:T(8,128)(2,1)S(1)} %copy-done.1), kind=kLoop, calls=%fused_computation.19 | loop fusion | flops 2621440 | bytes 5242880 | tf_op jit(solution)/shard_map/broadcast_in_dim | solution.py:125
  246.7 3.6 %add_bitcast_fusion.1 = f32[1,512,1024]{2,1,0:T(8,128)} fusion(bf16[512,1024]{1,0:T(8,128)(2,1)} %collective-permute-done.19, bf16[512,1024]{1,0:T(8,128)(2,1)} %collective-permute-done.17, bf16[1024,1024]{1,0:T(8,128)(2,1)S(1)} %copy-done.3), kind=kLoop, calls=%fused_computation.17 | loop fusion | flops 2621440 | bytes 5242880 | tf_op jit(solution)/shard_map/broadcast_in_dim | solution.py:125
  250.3 13.1 %collective-permute-done.22 = bf16[512,1024]{1,0:T(8,128)(2,1)S(1)} collective-permute-done((bf16[512,1024]{1,0:T(8,128)(2,1)S(1)}, bf16[512,1024]{1,0:T(8,128)(2,1)S(1)}, u32[]{:S(2)}, u32[]{:S(2)}) %collective-permute-start.22) | collective-permute-done | bytes 1048608 | tf_op jit(solution)/shard_map/ppermute | solution.py:92
  263.4 1.9 add_bitcast_fusion
  (121 shorter events, 12.6 us)
Async XLA Ops:
  5.2 11.5 %copy-start.10 = (bf16[192,1024]{1,0:T(8,128)(2,1)S(1)}, bf16[192,1024]{1,0:T(8,128)(2,1)}, u32[]{:S(2)}) copy-start(bf16[192,1024]{1,0:T(8,128)(2,1)} %param.15) | copy-start | bytes 1179652
  7.9 36.0 %all-to-all-start = ((bf16[8,72,1024]{2,1,0:T(8,128)(2,1)}), bf16[8,72,1024]{2,1,0:T(8,128)(2,1)}, u32[]{:S(2)}, u32[]{:S(2)}) async-start(bf16[8,72,1024]{2,1,0:T(8,128)(2,1)} %bitcast.2), calls=%async_computation | async-start | bytes 2359296 | tf_op jit(solution)/shard_map/all_to_all | solution.py:85
  15.2 3.1 %copy-start.24 = (f32[192,2]{0,1:T(2,128)S(1)}, f32[192,2]{0,1:T(2,128)}, u32[]{:S(2)}) copy-start(f32[192,2]{0,1:T(2,128)} %param.11) | copy-start | bytes 4612
  15.2 36.6 %collective-permute-start.4 = (bf16[512,1024]{1,0:T(8,128)(2,1)}, bf16[512,1024]{1,0:T(8,128)(2,1)}, u32[]{:S(2)}, u32[]{:S(2)}) collective-permute-start(bf16[512,1024]{1,0:T(8,128)(2,1)} %bitcast.6), channel_id=1, source_target_pairs={{0,16},{8,24},{16,0},{24,8},{1,17},{9,25},{17,1},{25,9},{2,18},{10... | collective-permute-start | bytes 3145736 | tf_op jit(solution)/shard_map/ppermute | solution.py:92
  43.8 62.6 %all-to-all-start.2 = ((bf16[8,72,1024]{2,1,0:T(8,128)(2,1)}), bf16[8,72,1024]{2,1,0:T(8,128)(2,1)S(1)}, u32[]{:S(2)}, u32[]{:S(2)}) async-start(bf16[8,72,1024]{2,1,0:T(8,128)(2,1)} %bitcast.10), calls=%async_computation.2 | async-start | bytes 2359296 | tf_op jit(solution)/shard_map/all_to_all | solution.py:86
  47.5 26.4 %collective-permute-start.2 = (bf16[512,1024]{1,0:T(8,128)(2,1)}, bf16[512,1024]{1,0:T(8,128)(2,1)}, u32[]{:S(2)}, u32[]{:S(2)}) collective-permute-start(bf16[512,1024]{1,0:T(8,128)(2,1)} %bitcast.5), channel_id=1, source_target_pairs={{0,16},{8,24},{16,0},{24,8},{1,17},{9,25},{17,1},{25,9},{2,18},{10... | collective-permute-start | bytes 3145736 | tf_op jit(solution)/shard_map/ppermute | solution.py:92
  49.0 46.1 %collective-permute-start = (bf16[512,1024]{1,0:T(8,128)(2,1)}, bf16[512,1024]{1,0:T(8,128)(2,1)}, u32[]{:S(2)}, u32[]{:S(2)}) collective-permute-start(bf16[512,1024]{1,0:T(8,128)(2,1)} %bitcast.4), channel_id=1, source_target_pairs={{0,16},{8,24},{16,0},{24,8},{1,17},{9,25},{17,1},{25,9},{2,18},{10... | collective-permute-start | bytes 3145736 | tf_op jit(solution)/shard_map/ppermute | solution.py:92
  49.5 46.8 %collective-permute-start.6 = (bf16[512,1024]{1,0:T(8,128)(2,1)}, bf16[512,1024]{1,0:T(8,128)(2,1)}, u32[]{:S(2)}, u32[]{:S(2)}) collective-permute-start(bf16[512,1024]{1,0:T(8,128)(2,1)} %bitcast.4), channel_id=1, source_target_pairs={{0,8},{8,0},{16,24},{24,16},{1,9},{9,1},{17,25},{25,17},{2,10},{10... | collective-permute-start | bytes 3145736 | tf_op jit(solution)/shard_map/ppermute | solution.py:95
  49.5 52.1 %collective-permute-start.7 = (bf16[512,1024]{1,0:T(8,128)(2,1)}, bf16[512,1024]{1,0:T(8,128)(2,1)}, u32[]{:S(2)}, u32[]{:S(2)}) collective-permute-start(bf16[512,1024]{1,0:T(8,128)(2,1)} %bitcast.5), channel_id=1, source_target_pairs={{0,8},{8,0},{16,24},{24,16},{1,9},{9,1},{17,25},{25,17},{2,10},{10... | collective-permute-start | bytes 3145736 | tf_op jit(solution)/shard_map/ppermute | solution.py:95
  51.8 54.7 %collective-permute-start.8 = (bf16[512,1024]{1,0:T(8,128)(2,1)}, bf16[512,1024]{1,0:T(8,128)(2,1)}, u32[]{:S(2)}, u32[]{:S(2)}) collective-permute-start(bf16[512,1024]{1,0:T(8,128)(2,1)} %bitcast.6), channel_id=1, source_target_pairs={{0,8},{8,0},{16,24},{24,16},{1,9},{9,1},{17,25},{25,17},{2,10},{10... | collective-permute-start | bytes 3145736 | tf_op jit(solution)/shard_map/ppermute | solution.py:95
  73.9 50.2 %collective-permute-start.5 = (bf16[512,1024]{1,0:T(8,128)(2,1)}, bf16[512,1024]{1,0:T(8,128)(2,1)}, u32[]{:S(2)}, u32[]{:S(2)}) collective-permute-start(bf16[512,1024]{1,0:T(8,128)(2,1)} %collective-permute-done.4), channel_id=1, source_target_pairs={{0,8},{8,0},{16,24},{24,16},{1,9},{9,1},{17,25},{25,17},{2,10},{10... | collective-permute-start | bytes 3145736 | tf_op jit(solution)/shard_map/ppermute | solution.py:95
  95.1 30.4 %collective-permute-start.3 = (bf16[512,1024]{1,0:T(8,128)(2,1)}, bf16[512,1024]{1,0:T(8,128)(2,1)}, u32[]{:S(2)}, u32[]{:S(2)}) collective-permute-start(bf16[512,1024]{1,0:T(8,128)(2,1)} %collective-permute-done.2), channel_id=1, source_target_pairs={{0,8},{8,0},{16,24},{24,16},{1,9},{9,1},{17,25},{25,17},{2,10},{10... | collective-permute-start | bytes 3145736 | tf_op jit(solution)/shard_map/ppermute | solution.py:95
  96.4 35.3 %collective-permute-start.1 = (bf16[512,1024]{1,0:T(8,128)(2,1)}, bf16[512,1024]{1,0:T(8,128)(2,1)}, u32[]{:S(2)}, u32[]{:S(2)}) collective-permute-start(bf16[512,1024]{1,0:T(8,128)(2,1)} %collective-permute-done), channel_id=1, source_target_pairs={{0,8},{8,0},{16,24},{24,16},{1,9},{9,1},{17,25},{25,17},{2,10},{10... | collective-permute-start | bytes 3145736 | tf_op jit(solution)/shard_map/ppermute | solution.py:95
  106.4 21.1 %copy-start.12 = (bf16[8,72,1024]{2,1,0:T(8,128)(2,1)}, bf16[8,72,1024]{2,1,0:T(8,128)(2,1)S(1)}, u32[]{:S(2)}) copy-start(bf16[8,72,1024]{2,1,0:T(8,128)(2,1)S(1)} %all-to-all-done.2) | copy-start | bytes 3538948
  113.1 3.4 %copy-start.26 = (bf16[576,1024]{1,0:T(8,128)(2,1)}, bf16[576,1024]{1,0:T(8,128)(2,1)S(1)}, u32[]{:S(2)}) copy-start(bf16[576,1024]{1,0:T(8,128)(2,1)S(1)} %get-tuple-element.11) | copy-start | bytes 3538948
  119.4 4.6 %copy-start.18 = (bf16[1024,1024]{1,0:T(8,128)(2,1)S(1)}, bf16[1024,1024]{1,0:T(8,128)(2,1)}, u32[]{:S(2)}) copy-start(bf16[1024,1024]{1,0:T(8,128)(2,1)} %constant_dynamic-update-slice_fusion.5) | copy-start | bytes 6291460
  124.0 1.9 copy-start.21
  125.5 3.5 %copy-start.19 = (bf16[1024,1024]{1,0:T(8,128)(2,1)}, bf16[1024,1024]{1,0:T(8,128)(2,1)S(1)}, u32[]{:S(2)}) copy-start(bf16[1024,1024]{1,0:T(8,128)(2,1)S(1)} %constant_dynamic-update-slice_fusion.4) | copy-start | bytes 6291460
  137.9 1.4 copy-start.29
  137.9 1.4 copy-start.14
  142.0 5.9 %copy-start.27 = (bf16[576,1024]{1,0:T(8,128)(2,1)S(1)}, bf16[576,1024]{1,0:T(8,128)(2,1)}, u32[]{:S(2)}) copy-start(bf16[576,1024]{1,0:T(8,128)(2,1)} %copy-done.26) | copy-start | bytes 3538948
  142.0 34.7 %all-to-all-start.3 = ((bf16[8,72,1024]{2,1,0:T(8,128)(2,1)}), bf16[8,72,1024]{2,1,0:T(8,128)(2,1)}, u32[]{:S(2)}, u32[]{:S(2)}) async-start(bf16[8,72,1024]{2,1,0:T(8,128)(2,1)} %bitcast.12), calls=%async_computation.3 | async-start | bytes 2359296 | tf_op jit(solution)/shard_map/all_to_all | solution.py:136
  147.8 3.3 %copy-start.1 = (bf16[1024,1024]{1,0:T(8,128)(2,1)S(1)}, bf16[1024,1024]{1,0:T(8,128)(2,1)}, u32[]{:S(2)}) copy-start(bf16[1024,1024]{1,0:T(8,128)(2,1)} %convolution_convert_fusion.5) | copy-start | bytes 6291460
  151.1 2.2 copy-start.2
  151.1 2.7 %copy-start.13 = (bf16[8,72,1024]{2,1,0:T(8,128)(2,1)S(1)}, bf16[8,72,1024]{2,1,0:T(8,128)(2,1)}, u32[]{:S(2)}) copy-start(bf16[8,72,1024]{2,1,0:T(8,128)(2,1)} %copy-done.12) | copy-start | bytes 3538948
  151.1 3.1 %copy-start.25 = (bf16[576,1024]{1,0:T(8,128)(2,1)S(1)}, bf16[576,1024]{1,0:T(8,128)(2,1)}, u32[]{:S(2)}) copy-start(bf16[576,1024]{1,0:T(8,128)(2,1)} %get-tuple-element.13) | copy-start | bytes 3538948
  152.2 61.5 %collective-permute-start.14 = (bf16[512,1024]{1,0:T(8,128)(2,1)}, bf16[512,1024]{1,0:T(8,128)(2,1)}, u32[]{:S(2)}, u32[]{:S(2)}) collective-permute-start(bf16[512,1024]{1,0:T(8,128)(2,1)} %slice.58), channel_id=1, source_target_pairs={{0,8},{8,0},{16,24},{24,16},{1,9},{9,1},{17,25},{25,17},{2,10},{10... | collective-permute-start | bytes 3145736 | tf_op jit(solution)/shard_map/ppermute | solution.py:95
  153.3 93.4 %collective-permute-start.17 = (bf16[512,1024]{1,0:T(8,128)(2,1)}, bf16[512,1024]{1,0:T(8,128)(2,1)}, u32[]{:S(2)}, u32[]{:S(2)}) collective-permute-start(bf16[512,1024]{1,0:T(8,128)(2,1)} %slice.62), channel_id=1, source_target_pairs={{0,8},{8,0},{16,24},{24,16},{1,9},{9,1},{17,25},{25,17},{2,10},{10... | collective-permute-start | bytes 3145736 | tf_op jit(solution)/shard_map/ppermute | solution.py:95
  156.1 4.2 %copy-start.4 = (bf16[1024,1024]{1,0:T(8,128)(2,1)}, bf16[1024,1024]{1,0:T(8,128)(2,1)S(1)}, u32[]{:S(2)}) copy-start(bf16[1024,1024]{1,0:T(8,128)(2,1)S(1)} %convolution_convert_fusion.1) | copy-start | bytes 6291460
  157.3 3.1 %copy-start.15 = (bf16[576,1024]{1,0:T(8,128)(2,1)S(1)}, bf16[576,1024]{1,0:T(8,128)(2,1)}, u32[]{:S(2)}) copy-start(bf16[576,1024]{1,0:T(8,128)(2,1)} %copy-done.14) | copy-start | bytes 3538948
  163.5 5.4 %copy-start.8 = (bf16[1024,1024]{1,0:T(8,128)(2,1)}, bf16[1024,1024]{1,0:T(8,128)(2,1)S(1)}, u32[]{:S(2)}) copy-start(bf16[1024,1024]{1,0:T(8,128)(2,1)S(1)} %convolution_convert_fusion.4) | copy-start | bytes 6291460
  163.5 2.1 copy-start.30
  164.5 23.4 %collective-permute-start.15 = (bf16[512,1024]{1,0:T(8,128)(2,1)}, bf16[512,1024]{1,0:T(8,128)(2,1)}, u32[]{:S(2)}, u32[]{:S(2)}) collective-permute-start(bf16[512,1024]{1,0:T(8,128)(2,1)} %slice.60), channel_id=1, source_target_pairs={{0,8},{8,0},{16,24},{24,16},{1,9},{9,1},{17,25},{25,17},{2,10},{10... | collective-permute-start | bytes 3145736 | tf_op jit(solution)/shard_map/ppermute | solution.py:95
  165.6 5.6 %copy-start.28 = (bf16[576,1024]{1,0:T(8,128)(2,1)S(1)}, bf16[576,1024]{1,0:T(8,128)(2,1)}, u32[]{:S(2)}) copy-start(bf16[576,1024]{1,0:T(8,128)(2,1)} %get-tuple-element.10) | copy-start | bytes 3538948
  168.9 1.3 copy-start.6
  170.2 2.0 copy-start.20
  171.2 22.8 %collective-permute-start.18 = (bf16[512,1024]{1,0:T(8,128)(2,1)}, bf16[512,1024]{1,0:T(8,128)(2,1)}, u32[]{:S(2)}, u32[]{:S(2)}) collective-permute-start(bf16[512,1024]{1,0:T(8,128)(2,1)} %slice.64), channel_id=1, source_target_pairs={{0,8},{8,0},{16,24},{24,16},{1,9},{9,1},{17,25},{25,17},{2,10},{10... | collective-permute-start | bytes 3145736 | tf_op jit(solution)/shard_map/ppermute | solution.py:95
  176.7 32.9 %all-to-all-start.1 = ((bf16[8,72,1024]{2,1,0:T(8,128)(2,1)}), bf16[8,72,1024]{2,1,0:T(8,128)(2,1)}, u32[]{:S(2)}, u32[]{:S(2)}) async-start(bf16[8,72,1024]{2,1,0:T(8,128)(2,1)} %bitcast.73), calls=%async_computation.1 | async-start | bytes 2359296 | tf_op jit(solution)/shard_map/all_to_all | solution.py:137
  184.3 1.0 copy-start.22
  184.4 3.2 %copy-start = (bf16[192,1024]{1,0:T(8,128)(2,1)S(1)}, bf16[192,1024]{1,0:T(8,128)(2,1)}, u32[]{:S(2)}) copy-start(bf16[192,1024]{1,0:T(8,128)(2,1)} %param.8) | copy-start | bytes 1179652
  184.4 3.2 %copy-start.23 = (f32[1024]{0:T(1024)S(1)}, f32[1024]{0:T(1024)}, u32[]{:S(2)}) copy-start(f32[1024]{0:T(1024)} %param.9) | copy-start | bytes 12292
  184.4 17.1 %collective-permute-start.21 = (bf16[512,1024]{1,0:T(8,128)(2,1)S(1)}, bf16[512,1024]{1,0:T(8,128)(2,1)S(1)}, u32[]{:S(2)}, u32[]{:S(2)}) collective-permute-start(bf16[512,1024]{1,0:T(8,128)(2,1)S(1)} %slice.68), channel_id=1, source_target_pairs={{0,8},{8,0},{16,24},{24,16},{1,9},{9,1},{17,25},{25,17},{2,10},{10... | collective-permute-start | bytes 3145736 | tf_op jit(solution)/shard_map/ppermute | solution.py:95
  185.3 4.6 %copy-start.9 = (bf16[1024,1024]{1,0:T(8,128)(2,1)S(1)}, bf16[1024,1024]{1,0:T(8,128)(2,1)}, u32[]{:S(2)}) copy-start(bf16[1024,1024]{1,0:T(8,128)(2,1)} %copy-done.8) | copy-start | bytes 6291460
  187.6 7.9 %copy-start.7 = (bf16[1024,1024]{1,0:T(8,128)(2,1)S(1)}, bf16[1024,1024]{1,0:T(8,128)(2,1)}, u32[]{:S(2)}) copy-start(bf16[1024,1024]{1,0:T(8,128)(2,1)} %copy-done.6) | copy-start | bytes 6291460
  187.9 4.6 %collective-permute-start.9 = (f32[8,128]{1,0:T(8,128)S(1)}, f32[8,128]{1,0:T(8,128)S(1)}, u32[]{:S(2)}, u32[]{:S(2)}) collective-permute-start(f32[8,128]{1,0:T(8,128)S(1)} %bitcast.74), channel_id=1, source_target_pairs={{0,1},{1,0},{2,3},{3,2},{4,5},{5,4},{6,7},{7,6},{8,9},{9,8},{10,11... | collective-permute-start | bytes 12296 | tf_op jit(solution)/shard_map/ppermute | solution.py:57
  192.5 50.6 %collective-permute-start.16 = (bf16[512,1024]{1,0:T(8,128)(2,1)}, bf16[512,1024]{1,0:T(8,128)(2,1)}, u32[]{:S(2)}, u32[]{:S(2)}) collective-permute-start(bf16[512,1024]{1,0:T(8,128)(2,1)} %add_convert_fusion.4), channel_id=1, source_target_pairs={{0,16},{8,24},{16,0},{24,8},{1,17},{9,25},{17,1},{25,9},{2,18},{10... | collective-permute-start | bytes 3145736 | tf_op jit(solution)/shard_map/ppermute | solution.py:92
  194.0 5.9 %collective-permute-start.10 = (f32[8,128]{1,0:T(8,128)S(1)}, f32[8,128]{1,0:T(8,128)S(1)}, u32[]{:S(2)}, u32[]{:S(2)}) collective-permute-start(f32[8,128]{1,0:T(8,128)S(1)} %bitcast_add_fusion), channel_id=1, source_target_pairs={{0,2},{1,3},{2,0},{3,1},{4,6},{5,7},{6,4},{7,5},{8,10},{9,11},{10,... | collective-permute-start | bytes 12296 | tf_op jit(solution)/shard_map/ppermute | solution.py:57
  200.0 46.8 %collective-permute-start.19 = (bf16[512,1024]{1,0:T(8,128)(2,1)}, bf16[512,1024]{1,0:T(8,128)(2,1)}, u32[]{:S(2)}, u32[]{:S(2)}) collective-permute-start(bf16[512,1024]{1,0:T(8,128)(2,1)} %add_convert_fusion.3), channel_id=1, source_target_pairs={{0,16},{8,24},{16,0},{24,8},{1,17},{9,25},{17,1},{25,9},{2,18},{10... | collective-permute-start | bytes 3145736 | tf_op jit(solution)/shard_map/ppermute | solution.py:92
  201.5 8.1 %collective-permute-start.11 = (f32[8,128]{1,0:T(8,128)S(1)}, f32[8,128]{1,0:T(8,128)S(1)}, u32[]{:S(2)}, u32[]{:S(2)}) collective-permute-start(f32[8,128]{1,0:T(8,128)S(1)} %fusion.71), channel_id=1, source_target_pairs={{0,4},{1,5},{2,6},{3,7},{4,0},{5,1},{6,2},{7,3},{8,12},{9,13},{10,... | collective-permute-start | bytes 12296 | tf_op jit(solution)/shard_map/ppermute | solution.py:57
  209.6 2.5 collective-permute-start.12
  209.6 4.1 %copy-start.17 = (bf16[512,1024]{1,0:T(8,128)(2,1)S(1)}, bf16[512,1024]{1,0:T(8,128)(2,1)}, u32[]{:S(2)}) copy-start(bf16[512,1024]{1,0:T(8,128)(2,1)} %slice.66) | copy-start | bytes 3145732
  209.6 30.2 %copy-start.16 = (bf16[512,1024]{1,0:T(8,128)(2,1)S(1)}, bf16[512,1024]{1,0:T(8,128)(2,1)}, u32[]{:S(2)}) copy-start(bf16[512,1024]{1,0:T(8,128)(2,1)} %add_convert_fusion.2) | copy-start | bytes 3145732
  209.6 31.7 %copy-start.11 = (bf16[192,1024]{1,0:T(8,128)(2,1)S(1)}, bf16[192,1024]{1,0:T(8,128)(2,1)}, u32[]{:S(2)}) copy-start(bf16[192,1024]{1,0:T(8,128)(2,1)} %param.15) | copy-start | bytes 1179652
  212.1 27.7 %collective-permute-start.13 = (f32[8,128]{1,0:T(8,128)S(1)}, f32[8,128]{1,0:T(8,128)S(1)}, u32[]{:S(2)}, u32[]{:S(2)}) collective-permute-start(f32[8,128]{1,0:T(8,128)S(1)} %add.113), channel_id=1, source_target_pairs={{0,16},{8,24},{16,0},{24,8},{1,17},{9,25},{17,1},{25,9},{2,18},{10... | collective-permute-start | bytes 12296 | tf_op jit(solution)/shard_map/ppermute | solution.py:57
  213.7 36.7 %collective-permute-start.20 = (bf16[512,1024]{1,0:T(8,128)(2,1)S(1)}, bf16[512,1024]{1,0:T(8,128)(2,1)S(1)}, u32[]{:S(2)}, u32[]{:S(2)}) collective-permute-start(bf16[512,1024]{1,0:T(8,128)(2,1)S(1)} %copy-done.17), channel_id=1, source_target_pairs={{0,8},{8,0},{16,24},{24,16},{1,9},{9,1},{17,25},{25,17},{2,10},{10... | collective-permute-start | bytes 3145736 | tf_op jit(solution)/shard_map/ppermute | solution.py:95
  239.8 23.6 %collective-permute-start.22 = (bf16[512,1024]{1,0:T(8,128)(2,1)S(1)}, bf16[512,1024]{1,0:T(8,128)(2,1)S(1)}, u32[]{:S(2)}, u32[]{:S(2)}) collective-permute-start(bf16[512,1024]{1,0:T(8,128)(2,1)S(1)} %copy-done.16), channel_id=1, source_target_pairs={{0,16},{8,24},{16,0},{24,8},{1,17},{9,25},{17,1},{25,9},{2,18},{10... | collective-permute-start | bytes 3145736 | tf_op jit(solution)/shard_map/ppermute | solution.py:92
  243.1 3.6 %copy-start.3 = (bf16[1024,1024]{1,0:T(8,128)(2,1)S(1)}, bf16[1024,1024]{1,0:T(8,128)(2,1)}, u32[]{:S(2)}) copy-start(bf16[1024,1024]{1,0:T(8,128)(2,1)} %copy-done.2) | copy-start | bytes 6291460
  246.7 16.7 %copy-start.5 = (bf16[1024,1024]{1,0:T(8,128)(2,1)S(1)}, bf16[1024,1024]{1,0:T(8,128)(2,1)}, u32[]{:S(2)}) copy-start(bf16[1024,1024]{1,0:T(8,128)(2,1)} %copy-done.4) | copy-start | bytes 6291460
